TPU v7x, 32 devices: a whole 2x2x4 slice. The times are simulated.
32 devices in a mesh: expert: 8 (over z, y), blk: 4 (over x, core).
Axes of the slice: x: 2, y: 2, z: 4, core: 2. Of those that a mesh axis runs over, the one named last changes fastest.
Arguments:
- inputs: bfloat16 [8, 768, 1536], P('expert', 'blk'), may hold values from -6 to 6
- output_grads: bfloat16 [8, 768, 4096], P('expert', 'blk'), may hold values from -0.21875 to 0.21875
- route_counts: int32 [8, 4], P('expert', 'blk'), may hold values from 48 to 192, as said below
- left_rows: bfloat16 [8, 2304, 1536], P(None, 'expert', 'blk'), as said below
- left_lengths: int32 [8, 8], replicated, may hold values from 96 to 288, as said below
- right_inverse: bfloat16 [8, 4096, 4096], P('expert', 'blk'), may hold values from -0.09375 to 0.09375
Outputs:
- preconditioned: float32 [8, 4096, 1536], P('expert', 'blk')
Inputs may be any that keep to these rules, and one draw needn't show every extreme that they name: `route_counts`: for every expert, one device of blk holds exactly 192 routed tokens and one holds exactly 48. `left_lengths`: each row sums to 1536; in each row one owner holds exactly 288 rows and one exactly 96. `left_rows`: slots i * 288 + j with j >= left_lengths[e, i] are zero.
All inputs are finite; a program needn't handle non-finite values.
Results may differ from a plain program's by a relative error of at most 0.0041.
Values may be sent and summed in bfloat16 or wider, within the bound.
A program may use at most 128 MiB of HBM per device.

v0:
```python
import jax
import jax.numpy as jnp
from jax import lax
from jax.sharding import PartitionSpec as P


def shards(inputs, output_grads, route_counts, left_rows, left_lengths, right_inverse):
    token_rows = inputs[0]
    grad_rows = output_grads[0]
    slot_count = token_rows.shape[0]
    width_in = token_rows.shape[1]
    live_rows = lax.broadcasted_iota(jnp.int32, (slot_count, 1), 0) < route_counts[0, 0]
    masked = jnp.where(live_rows, token_rows, jnp.zeros_like(token_rows))
    contract_rows = (((0,), (0,)), ((), ()))
    columns = lax.all_to_all(grad_rows, "blk", split_axis=1, concat_axis=0, tiled=True)
    gradient = lax.dot_general(
        columns,
        lax.all_gather(masked, "blk", axis=0, tiled=True),
        contract_rows,
        preferred_element_type=jnp.float32,
    )
    gradient = gradient.astype(jnp.bfloat16)
    own_expert = lax.axis_index("expert")
    lengths = lax.dynamic_index_in_dim(left_lengths, own_expert, 0, keepdims=False)
    starts = jnp.cumsum(lengths) - lengths
    owners = lengths.shape[0]
    piece_slots = left_rows.shape[1]
    offset = lax.broadcasted_iota(jnp.int32, (owners, piece_slots), 1)
    row_index = jnp.minimum(starts[:, None] + offset, width_in - 1).reshape(owners * piece_slots)
    kept_rows = (offset < lengths[:, None]).reshape(1, owners * piece_slots)
    picked = jnp.where(
        kept_rows, jnp.take(gradient, row_index, axis=1), jnp.zeros((), jnp.bfloat16)
    )
    arrived = lax.all_to_all(left_rows, "expert", split_axis=0, concat_axis=1, tiled=True)
    weighted = jnp.dot(
        picked,
        lax.all_gather(arrived, "blk", axis=2, tiled=True)[0],
        preferred_element_type=jnp.float32,
    ).astype(jnp.bfloat16)
    inverse_rows = right_inverse[0]
    everything = lax.all_gather(weighted, "blk", axis=0, tiled=True)
    result = jnp.dot(inverse_rows, everything, preferred_element_type=jnp.float32)
    return result[None]


def solution(mesh):
    in_specs = (
        P("expert", "blk", None),
        P("expert", "blk", None),
        P("expert", "blk"),
        P(None, "expert", "blk"),
        P(),
        P("expert", "blk", None),
    )
    out_specs = P("expert", "blk", None)
    return jax.shard_map(shards, mesh=mesh, in_specs=in_specs, out_specs=out_specs, check_vma=False)
```

profile of v0, /device:TPU:0, one launch (start us, length us, event | category | flops | bytes accessed | tf_op | source)
XLA Modules:
  0.0 251.2 jit_solution(289022120514469136)
XLA Ops:
  6.5 0.0 copy-start
  6.5 0.0 all-gather.4.cloned.1.call-start
  7.3 2.0 bitcast_select_fusion
  9.3 0.0 all-gather.4.cloned.1.call-update
  9.3 0.0 all-gather.6.cloned.1.call-start
  9.4 48.7 %all_to_all.31 = bf16[8,288,384]{2,1,0:T(8,128)(2,1)} all-to-all(bf16[8,288,384]{2,1,0:T(8,128)(2,1)} %param.9), channel_id=1, replica_groups=mesh['expert'=8,'blk'=4] {'expert'}, dimensions={0} | all-to-all | bytes 3538944 | tf_op jit(solution)/shard_map/all_to_all | solution.py:34
  58.1 0.0 all-gather.6.cloned.1.call-update
  58.1 0.0 copy-done
  58.1 1.2 all_to_all.23
  59.3 1.6 copy.11
  60.9 3.6 %all-to-all-start = ((bf16[192,4,1024]{2,0,1:T(8,128)(2,1)}), bf16[192,4,1024]{2,0,1:T(8,128)(2,1)S(1)}, u32[]{:S(2)}, u32[]{:S(2)}) async-start(bf16[192,4,1024]{2,0,1:T(8,128)(2,1)} %copy.11), calls=%async_computation | async-start | bytes 3145728 | tf_op jit(solution)/shard_map/all_to_all | solution.py:15
  64.5 0.0 all-gather.8.cloned.1.call-start
  64.6 0.7 fusion.20
  65.3 0.2 reduce-window.8
  65.5 0.7 bitcast_subtract_fusion
  66.2 0.1 add_minimum_fusion
  66.3 0.1 min.28
  66.3 0.1 min.26
  66.4 0.1 iota_compare_fusion
  66.5 0.1 lt.57
  66.7 34.6 %all-to-all-done = bf16[192,4,1024]{2,0,1:T(8,128)(2,1)S(1)} async-done(((bf16[192,4,1024]{2,0,1:T(8,128)(2,1)}), bf16[192,4,1024]{2,0,1:T(8,128)(2,1)S(1)}, u32[]{:S(2)}, u32[]{:S(2)}) %all-to-all-start) | async-done | bytes 1572896 | tf_op jit(solution)/shard_map/all_to_all | solution.py:15
  101.2 0.0 copy-start.1
  101.2 0.0 all-gather.4.cloned.1.call-done
  101.2 1.1 copy-done.1
  102.4 4.8 %fusion.16 = bf16[1024,1536]{0,1:T(8,128)(2,1)S(1)} fusion(bf16[768,1536]{1,0:T(8,128)(2,1)} %all-gather.4.cloned.1.call-done, bf16[768,1024]{1,0:T(8,128)(2,1)} %bitcast.35), kind=kOutput, calls=%fused_computation.12 | convolution fusion | flops 2417491968 | bytes 7077888 | tf_op jit(solution)/shard_map/dot_general | solution.py:16
  107.1 8.1 %gather_fusion = bf16[2304,1024]{1,0:T(8,128)(2,1)} fusion(bf16[1024,1536]{0,1:T(8,128)(2,1)S(1)} %fusion.16, s32[3072]{0:T(1024)S(1)} %pad_clamp_fusion), kind=kCustom, calls=%fused_computation | custom fusion | bytes 9446400 | tf_op jit(solution)/shard_map/jit(_take)/gather | solution.py:32
  115.2 8.9 %all-gather.6.cloned.1.call-done = bf16[1,2304,1536]{2,1,0:T(8,128)(2,1)} async-done(((bf16[1,2304,384]{2,1,0:T(8,128)(2,1)}), bf16[1,2304,1536]{2,1,0:T(8,128)(2,1)}) %all-gather.6.cloned.1.call-update) | async-done | bytes 7077904 | tf_op jit(solution)/shard_map/all_gather | solution.py:37
  124.1 14.1 %fusion.11 = bf16[1024,1536]{1,0:T(8,128)(2,1)} fusion(bf16[1,2304,1536]{2,1,0:T(8,128)(2,1)} %all-gather.6.cloned.1.call-done, bf16[2304,1024]{1,0:T(8,128)(2,1)} %gather_fusion, pred[2304]{0:T(1024)(128)(4,1)S(1)} %lt.57, pred[2304]{0:T(1024)(128)(4,1)S(1)} %compare_and_fusion), kind=kOutput, calls=%fused_computation.10 | convolution fusion | flops 7254048768 | bytes 14946816 | tf_op jit(solution)/shard_map/dot_general | solution.py:35
  138.2 0.0 all-gather.8.cloned.1.call-update
  138.3 80.2 %all-gather.8.cloned.1.call-done = bf16[4096,1536]{1,0:T(8,128)(2,1)} async-done(((bf16[1024,1536]{1,0:T(8,128)(2,1)}), bf16[4096,1536]{1,0:T(8,128)(2,1)}) %all-gather.8.cloned.1.call-update) | async-done | bytes 12582928 | tf_op jit(solution)/shard_map/all_gather | solution.py:41
  218.5 19.7 %fusion.8 = f32[1,1024,1536]{1,2,0:T(8,128)} fusion(bf16[4096,1536]{1,0:T(8,128)(2,1)} %all-gather.8.cloned.1.call-done, bf16[1,1024,4096]{2,1,0:T(8,128)(2,1)} %param.11), kind=kOutput, calls=%fused_computation.9 | convolution fusion | flops 12884901888 | bytes 27262976 | tf_op jit(solution)/shard_map/dot_general | solution.py:42
  238.2 6.6 %copy.12 = f32[1,1024,1536]{2,1,0:T(8,128)} copy(f32[1,1024,1536]{1,2,0:T(8,128)} %fusion.8) | data formatting | bytes 12582912 | tf_op jit(solution)/shard_map/broadcast_in_dim | solution.py:43
  (4 shorter events, 0.1 us)
Async XLA Ops:
  6.5 51.6 %copy-start = (bf16[1,192,4096]{2,1,0:T(8,128)(2,1)S(1)}, bf16[1,192,4096]{2,1,0:T(8,128)(2,1)}, u32[]{:S(2)}) copy-start(bf16[1,192,4096]{2,1,0:T(8,128)(2,1)} %param.7) | copy-start | bytes 4718596
  6.5 94.7 %all-gather.4.cloned.1.call-start = ((), (), s32[]{:S(2)}) async-start(), calls=%async_computation.2 | async-start | bytes 2949120 | tf_op jit(solution)/shard_map/all_gather | solution.py:18
  9.3 114.8 %all-gather.6.cloned.1.call-start = ((), (), s32[]{:S(2)}) async-start(), calls=%async_computation.3 | async-start | bytes 8847360 | tf_op jit(solution)/shard_map/all_gather | solution.py:37
  60.9 40.3 %all-to-all-start = ((bf16[192,4,1024]{2,0,1:T(8,128)(2,1)}), bf16[192,4,1024]{2,0,1:T(8,128)(2,1)S(1)}, u32[]{:S(2)}, u32[]{:S(2)}) async-start(bf16[192,4,1024]{2,0,1:T(8,128)(2,1)} %copy.11), calls=%async_computation | async-start | bytes 3145728 | tf_op jit(solution)/shard_map/all_to_all | solution.py:15
  64.5 153.9 %all-gather.8.cloned.1.call-start = ((), (), s32[]{:S(2)}) async-start(), calls=%async_computation.4 | async-start | bytes 15728640 | tf_op jit(solution)/shard_map/all_gather | solution.py:41
  101.2 1.1 copy-start.1
Sparse Core Ops, SparseCore 0:
  9.5 26.7 all-gather.3
  58.2 65.8 all-gather.5
  138.4 80.0 all-gather.7
where the time goes:
time: 252 us; the launch traced here: 251 us
  waiting for transfers between devices  124 us (49%)
  blocking collectives  48.7 us (19%)
  matrix products  38.6 us (15%)
  local copies, waits for them, and re-layouts  19.5 us (8%)
  between operations  13.9 us (6%)
  starting transfers between devices  3.7 us (1%)
  other arithmetic  3.08 us (1%)
    all_gather x1, waiting for transfers between devices, shards(): everything = lax.all_gather(weighted, 'blk', axis=0, tiled=True)  80.2 us
    all_to_all x1, blocking collectives, shards(): lax.all_to_all(left_rows, 'expert', split_axis=0, concat_axis=1, tiled=True)  48.7 us
    all_to_all x1, waiting for transfers between devices, shards(): lax.all_to_all(grad_rows, 'blk', split_axis=1, concat_axis=0, tiled=True)  34.6 us
    dot_general x1, matrix products, shards(): jnp.dot(inverse_rows, everything, preferred_element_type=jnp.float32)  19.7 us
    dot_general x1, matrix products, shards(): jnp.dot(picked, lax.all_gather(arrived, 'blk', axis=2, tiled=True)[0], pr...  14.1 us
    all_gather x1, waiting for transfers between devices, shards(): lax.all_gather(arrived, 'blk', axis=2, tiled=True)[0]  8.9 us
    gather x1, local copies, waits for them, and re-layouts, shards(): jnp.take(gradient, row_index, axis=1)  8.06 us
    broadcast_in_dim x1, local copies, waits for them, and re-layouts, shards(): return result[None]  6.56 us
  transfers between devices with their start and end apart: 4, of which 3 were waited for; matrix products, arithmetic and copies ran while one was open for 7% of the time, Pallas kernels for 0%

commit v1 on v0

--- a/solution.py
+++ b/solution.py
@@ -12,7 +12,18 @@
     live_rows = lax.broadcasted_iota(jnp.int32, (slot_count, 1), 0) < route_counts[0, 0]
     masked = jnp.where(live_rows, token_rows, jnp.zeros_like(token_rows))
     contract_rows = (((0,), (0,)), ((), ()))
-    columns = lax.all_to_all(grad_rows, "blk", split_axis=1, concat_axis=0, tiled=True)
+    ways, here = (lax.axis_size("blk"), lax.axis_index("blk"))
+    width = grad_rows.shape[1] // ways
+    lengths_2 = list(grad_rows.shape)
+    lengths_2[1] = width
+    height = lengths_2[0]
+    lengths_2[0] = height * ways
+    columns = jnp.zeros(lengths_2, grad_rows.dtype)
+    for mask in range(ways):
+        part = lax.dynamic_slice_in_dim(grad_rows, (here ^ mask) * width, width, axis=1)
+        if mask:
+            part = lax.ppermute(part, "blk", [(d, d ^ mask) for d in range(ways)])
+        columns = lax.dynamic_update_slice_in_dim(columns, part, (here ^ mask) * height, axis=0)
     gradient = lax.dot_general(
         columns,
         lax.all_gather(masked, "blk", axis=0, tiled=True),

time: 252 us -> 246 us (0.976)
  waiting for transfers between devices: 124 us -> 113 us
  local copies, waits for them, and re-layouts: 19.5 us -> 22.9 us
  other arithmetic: 3.08 us -> 6.13 us
    all_to_all x1 -> x0, waiting for transfers between devices: 34.6 us -> none  [shards(): lax.all_to_all(grad_rows, 'blk', split_axis=1, concat_axis=0, tiled=True)]
    ppermute x0 -> x3, waiting for transfers between devices: none -> 16.7 us  [shards(): part = lax.ppermute(part, 'blk', [(d, d ^ mask) for d in range(ways)])]
    all_gather x1, waiting for transfers between devices: 8.9 us -> 15.3 us  [shards(): lax.all_gather(arrived, 'blk', axis=2, tiled=True)[0]]
    dynamic_update_slice x0 -> x4, local copies, waits for them, and re-layouts: none -> 4.1 us  [shards(): lax.dynamic_update_slice_in_dim(columns, part, (here ^ mask) * height, ax...]
    all_to_all x1 -> x0, starting transfers between devices: 3.61 us -> none  [shards(): lax.all_to_all(grad_rows, 'blk', split_axis=1, concat_axis=0, tiled=True)]
    all_to_all x2 -> x0, local copies, waits for them, and re-layouts: 2.8 us -> none  [shards(): lax.all_to_all(grad_rows, 'blk', split_axis=1, concat_axis=0, tiled=True)]
  transfers between devices with their start and end apart: 4 -> 6, of which waited for: 3 -> 3; matrix products, arithmetic and copies ran while one was open for 7% -> 10% of each run, Pallas kernels for 0% -> 0%
where the time goes in v1:
time: 246 us
  waiting for transfers between devices  113 us (46%)
  blocking collectives  48.8 us (20%)
  matrix products  38.6 us (16%)
  local copies, waits for them, and re-layouts  22.9 us (9%)
  between operations  13.9 us (6%)
  other arithmetic  6.13 us (2%)
    all_gather x1, waiting for transfers between devices, shards(): everything = lax.all_gather(weighted, 'blk', axis=0, tiled=True)  80.9 us
    all_to_all x1, blocking collectives, shards(): lax.all_to_all(left_rows, 'expert', split_axis=0, concat_axis=1, tiled=True)  48.8 us
    dot_general x1, matrix products, shards(): jnp.dot(inverse_rows, everything, preferred_element_type=jnp.float32)  19.7 us
    ppermute x3, waiting for transfers between devices, shards(): part = lax.ppermute(part, 'blk', [(d, d ^ mask) for d in range(ways)])  16.7 us
    all_gather x1, waiting for transfers between devices, shards(): lax.all_gather(arrived, 'blk', axis=2, tiled=True)[0]  15.3 us
    dot_general x1, matrix products, shards(): jnp.dot(picked, lax.all_gather(arrived, 'blk', axis=2, tiled=True)[0], pr...  14.1 us
    gather x1, local copies, waits for them, and re-layouts, shards(): jnp.take(gradient, row_index, axis=1)  8.06 us
    broadcast_in_dim x1, local copies, waits for them, and re-layouts, shards(): return result[None]  6.56 us
  transfers between devices with their start and end apart: 6, of which 3 were waited for; matrix products, arithmetic and copies ran while one was open for 10% of the time, Pallas kernels for 0%

profile of v1, /device:TPU:0, one launch (start us, length us, event | category | flops | bytes accessed | tf_op | source)
XLA Modules:
  0.0 245.6 jit_solution(5899055387340232381)
XLA Ops:
  7.2 2.0 bitcast_select_fusion
  9.2 0.0 all-gather.6.cloned.1.call-start
  9.3 48.8 %all_to_all.12 = bf16[8,288,384]{2,1,0:T(8,128)(2,1)} all-to-all(bf16[8,288,384]{2,1,0:T(8,128)(2,1)} %param.9), channel_id=1, replica_groups=mesh['expert'=8,'blk'=4] {'expert'}, dimensions={0} | all-to-all | bytes 3538944 | tf_op jit(solution)/shard_map/all_to_all | solution.py:45
  58.1 0.0 all-gather.6.cloned.1.call-update
  58.1 0.0 all-gather.8.cloned.1.call-start
  58.2 0.1 dynamic-slice_bitcast_fusion
  58.3 0.1 collective-permute-start.2
  58.4 1.6 collective-permute-start
  60.0 0.5 collective-permute-start.1
  60.5 0.7 fusion.19
  61.2 0.2 reduce-window.8
  61.4 1.2 bitcast_subtract_fusion
  62.6 0.1 add_minimum_fusion
  62.7 0.7 min.26
  63.3 1.3 compare_and_fusion
  64.6 0.6 iota_compare_fusion
  65.3 0.7 min.28
  66.0 0.7 fusion.18
  66.7 0.7 lt.81
  67.4 1.3 broadcast_in_dim.43
  68.8 0.8 bitcast_dynamic-update-slice_fusion
  69.6 1.8 constant_dynamic-update-slice_fusion.2
  71.3 16.7 %collective-permute-done.1 = bf16[192,1024]{1,0:T(8,128)(2,1)S(1)} collective-permute-done((bf16[192,1024]{1,0:T(8,128)(2,1)S(1)}, bf16[192,1024]{1,0:T(8,128)(2,1)S(1)}, u32[]{:S(2)}, u32[]{:S(2)}) %collective-permute-start.1) | collective-permute-done | bytes 393248 | tf_op jit(solution)/shard_map/ppermute | solution.py:25
  88.1 0.8 constant_dynamic-update-slice_fusion.1
  88.8 0.8 constant_dynamic-update-slice_fusion
  89.6 4.8 %convolution_convert_fusion = bf16[1024,1536]{0,1:T(8,128)(2,1)S(1)} fusion(bf16[768,1024]{1,0:T(8,128)(2,1)} %constant_dynamic-update-slice_fusion, bf16[768,1536]{1,0:T(8,128)(2,1)} %all-gather.4.cloned.1.call-done), kind=kOutput, calls=%fused_computation.11 | convolution fusion | flops 2417491968 | bytes 7077888 | tf_op jit(solution)/shard_map/dot_general | solution.py:27
  94.4 8.1 %gather_fusion = bf16[2304,1024]{1,0:T(8,128)(2,1)} fusion(bf16[1024,1536]{0,1:T(8,128)(2,1)S(1)} %convolution_convert_fusion, s32[3072]{0:T(1024)S(1)} %pad_clamp_fusion), kind=kCustom, calls=%fused_computation | custom fusion | bytes 9446400 | tf_op jit(solution)/shard_map/jit(_take)/gather | solution.py:43
  102.5 15.3 %all-gather.6.cloned.1.call-done = bf16[1,2304,1536]{2,1,0:T(8,128)(2,1)} async-done(((bf16[1,2304,384]{2,1,0:T(8,128)(2,1)}), bf16[1,2304,1536]{2,1,0:T(8,128)(2,1)}) %all-gather.6.cloned.1.call-update) | async-done | bytes 7077904 | tf_op jit(solution)/shard_map/all_gather | solution.py:48
  117.8 14.1 %fusion.11 = bf16[1024,1536]{1,0:T(8,128)(2,1)} fusion(bf16[1,2304,1536]{2,1,0:T(8,128)(2,1)} %all-gather.6.cloned.1.call-done, bf16[2304,1024]{1,0:T(8,128)(2,1)} %gather_fusion, pred[2304]{0:T(1024)(128)(4,1)S(1)} %copy-done.1, pred[2304]{0:T(1024)(128)(4,1)S(1)} %copy-done.2), kind=kOutput, calls=%fused_computation.10 | convolution fusion | flops 7254048768 | bytes 14946816 | tf_op jit(solution)/shard_map/dot_general | solution.py:46
  132.0 80.9 %all-gather.8.cloned.1.call-done = bf16[4096,1536]{1,0:T(8,128)(2,1)} async-done(((bf16[1024,1536]{1,0:T(8,128)(2,1)}), bf16[4096,1536]{1,0:T(8,128)(2,1)}) %all-gather.8.cloned.1.call-update) | async-done | bytes 12582928 | tf_op jit(solution)/shard_map/all_gather | solution.py:52
  212.9 19.7 %fusion.8 = f32[1,1024,1536]{1,2,0:T(8,128)} fusion(bf16[4096,1536]{1,0:T(8,128)(2,1)} %all-gather.8.cloned.1.call-done, bf16[1,1024,4096]{2,1,0:T(8,128)(2,1)} %param.11), kind=kOutput, calls=%fused_computation.9 | convolution fusion | flops 12884901888 | bytes 27262976 | tf_op jit(solution)/shard_map/dot_general | solution.py:53
  232.5 6.6 %copy.7 = f32[1,1024,1536]{2,1,0:T(8,128)} copy(f32[1,1024,1536]{1,2,0:T(8,128)} %fusion.8) | data formatting | bytes 12582912 | tf_op jit(solution)/shard_map/broadcast_in_dim | solution.py:54
  (14 shorter events, 0.1 us)
Async XLA Ops:
  6.5 83.1 %all-gather.4.cloned.1.call-start = ((), (), s32[]{:S(2)}) async-start(), calls=%async_computation.1 | async-start | bytes 2949120 | tf_op jit(solution)/shard_map/all_gather | solution.py:29
  9.2 49.0 %copy-start = (bf16[1,192,4096]{2,1,0:T(8,128)(2,1)S(1)}, bf16[1,192,4096]{2,1,0:T(8,128)(2,1)}, u32[]{:S(2)}) copy-start(bf16[1,192,4096]{2,1,0:T(8,128)(2,1)} %param.7) | copy-start | bytes 4718596
  9.2 108.6 %all-gather.6.cloned.1.call-start = ((), (), s32[]{:S(2)}) async-start(), calls=%async_computation.2 | async-start | bytes 8847360 | tf_op jit(solution)/shard_map/all_gather | solution.py:48
  58.1 154.8 %all-gather.8.cloned.1.call-start = ((), (), s32[]{:S(2)}) async-start(), calls=%async_computation.3 | async-start | bytes 15728640 | tf_op jit(solution)/shard_map/all_gather | solution.py:52
  58.3 30.5 %collective-permute-start.2 = (bf16[192,1024]{1,0:T(8,128)(2,1)S(1)}, bf16[192,1024]{1,0:T(8,128)(2,1)S(1)}, u32[]{:S(2)}, u32[]{:S(2)}) collective-permute-start(bf16[192,1024]{1,0:T(8,128)(2,1)S(1)} %get-tuple-element.7), channel_id=1, source_target_pairs={{0,3},{1,2},{2,1},{3,0},{4,7},{5,6},{6,5},{7,4},{8,11},{9,10},{10,... | collective-permute-start | bytes 1179656 | tf_op jit(solution)/shard_map/ppermute | solution.py:25
  58.4 11.1 %collective-permute-start = (bf16[192,1024]{1,0:T(8,128)(2,1)S(1)}, bf16[192,1024]{1,0:T(8,128)(2,1)}, u32[]{:S(2)}, u32[]{:S(2)}) collective-permute-start(bf16[192,1024]{1,0:T(8,128)(2,1)S(1)} %get-tuple-element.8), channel_id=1, source_target_pairs={{0,1},{1,0},{2,3},{3,2},{4,5},{5,4},{6,7},{7,6},{8,9},{9,8},{10,11... | collective-permute-start | bytes 1179656 | tf_op jit(solution)/shard_map/ppermute | solution.py:25
  60.0 28.1 %collective-permute-start.1 = (bf16[192,1024]{1,0:T(8,128)(2,1)S(1)}, bf16[192,1024]{1,0:T(8,128)(2,1)S(1)}, u32[]{:S(2)}, u32[]{:S(2)}) collective-permute-start(bf16[192,1024]{1,0:T(8,128)(2,1)S(1)} %get-tuple-element.9), channel_id=1, source_target_pairs={{0,2},{1,3},{2,0},{3,1},{4,6},{5,7},{6,4},{7,5},{8,10},{9,11},{10,... | collective-permute-start | bytes 1179656 | tf_op jit(solution)/shard_map/ppermute | solution.py:25
  94.4 23.4 %copy-start.1 = (pred[2304]{0:T(1024)(128)(4,1)S(1)}, pred[2304]{0:T(1024)(128)(4,1)}, u32[]{:S(2)}) copy-start(pred[2304]{0:T(1024)(128)(4,1)} %lt.81) | copy-start | bytes 6916
  94.4 23.4 %copy-start.2 = (pred[2304]{0:T(1024)(128)(4,1)S(1)}, pred[2304]{0:T(1024)(128)(4,1)}, u32[]{:S(2)}) copy-start(pred[2304]{0:T(1024)(128)(4,1)} %compare_and_fusion) | copy-start | bytes 6916
Sparse Core Ops, SparseCore 0:
  9.3 26.7 all-gather.3
  58.2 59.4 all-gather.5
  132.1 80.7 all-gather.7
